TPU v7x, 256 devices: a whole 4x4x8 slice. The times are simulated.
256 devices in a mesh: seq: 32 (over z, x), head: 8 (over y, core).
Axes of the slice: x: 4, y: 4, z: 8, core: 2. Of those that a mesh axis runs over, the one named last changes fastest.
Arguments:
- queries: bfloat16 [16384, 1024], P(('seq', 'head')), may hold values from -24 to 24
- keys: bfloat16 [16384, 1024], P(('seq', 'head')), may hold values from -6 to 6
- values: bfloat16 [16384, 1024], P(('seq', 'head')), may hold values from -6 to 6
- out_grad: bfloat16 [16384, 1024], P(('seq', 'head')), may hold values from -6 to 6
- key_blocks: int32 [128, 8], replicated, may hold values from 0 to 127, as said below
- counts: int32 [128], replicated, may hold values from 2 to 8, as said below
Outputs:
- attention: bfloat16 [16384, 1024], P('seq', 'head')
- query_grad: bfloat16 [16384, 1024], P('seq', 'head')
- key_grad: bfloat16 [16384, 1024], P('seq', 'head')
- value_grad: bfloat16 [16384, 1024], P('seq', 'head')
Inputs may be any that keep to these rules, and one draw needn't show every extreme that they name: `counts`: some query block uses all 8 listed blocks. `key_blocks`: row a lists 8 different blocks, the first being block a itself and the second block (a - 1) modulo 128; only the first counts[a] of them are used.
All inputs are finite; a program needn't handle non-finite values.
Results may differ from a plain program's by a relative error of at most 0.015.
Values may be sent and summed in bfloat16 or wider, within the bound.
A program may use at most 64 MiB of HBM per device.

v0:
```python
import math
import jax
import jax.numpy as jnp
from jax import lax
from jax.sharding import PartitionSpec as P

HEADS = 8
BLK = 128
neg_fill = -1e30
tile_limit = 512


def block_table(key_blocks, counts):
    block_count = key_blocks.shape[0]
    slot_ids = jnp.arange(key_blocks.shape[1])
    live_slot = slot_ids[None, :] < counts[:, None]
    matches = (key_blocks[:, :, None] == jnp.arange(block_count)[None, None, :]) & live_slot[
        :, :, None
    ]
    return jnp.any(matches, axis=1).astype(jnp.float32)


def one_hot_rows(first_row, row_total, block_count):
    block_ids = (first_row + jnp.arange(row_total)) // BLK
    return (block_ids[:, None] == jnp.arange(block_count)[None, :]).astype(jnp.float32)


def on_device(queries, keys, values, out_grad, key_blocks, counts):
    heads_here = HEADS // lax.axis_size("head")
    q_rows, k_rows, v_rows, g_rows = (
        lax.all_to_all(queries, "head", split_axis=1, concat_axis=0, tiled=True),
        lax.all_to_all(keys, "head", split_axis=1, concat_axis=0, tiled=True),
        lax.all_to_all(values, "head", split_axis=1, concat_axis=0, tiled=True),
        lax.all_to_all(out_grad, "head", split_axis=1, concat_axis=0, tiled=True),
    )
    row_count = q_rows.shape[0]
    feat_width = q_rows.shape[1]
    head_dim = feat_width // heads_here
    score_scale = 1.0 / math.sqrt(head_dim)
    block_count = key_blocks.shape[0]
    slot_total = key_blocks.shape[1]
    local_blocks = row_count // BLK
    first_block = lax.axis_index("seq") * local_blocks
    listed = lax.dynamic_slice_in_dim(key_blocks, first_block, local_blocks, 0)
    used = lax.dynamic_slice_in_dim(counts, first_block, local_blocks, 0)
    slot_ids = jnp.arange(slot_total)
    live = jnp.repeat(slot_ids[None, :] < used[:, None], BLK, axis=1)
    live_mask = live[:, None, None, :]

    def listed_sets(k_whole, v_whole):
        k_blocks = k_whole.reshape(block_count, BLK, heads_here, head_dim)
        v_blocks = v_whole.reshape(block_count, BLK, heads_here, head_dim)
        key_set = jnp.take(k_blocks, listed, axis=0).reshape(
            local_blocks, slot_total * BLK, heads_here, head_dim
        )
        value_set = jnp.take(v_blocks, listed, axis=0).reshape(
            local_blocks, slot_total * BLK, heads_here, head_dim
        )
        return (key_set, value_set)

    q_blocks = q_rows.reshape(local_blocks, BLK, heads_here, head_dim)
    g_blocks = g_rows.reshape(local_blocks, BLK, heads_here, head_dim)

    def block_scores(key_set):
        scores = (
            jnp.einsum("bqhd,bkhd->bhqk", q_blocks, key_set, preferred_element_type=jnp.float32)
            * score_scale
        )
        return jnp.where(live_mask, scores, neg_fill)

    k_whole, v_whole = (
        lax.all_gather(k_rows, "seq", axis=0, tiled=True),
        lax.all_gather(v_rows, "seq", axis=0, tiled=True),
    )
    key_set, value_set = listed_sets(k_whole, v_whole)
    scores = block_scores(key_set)
    row_max = jnp.max(scores, axis=3)
    weights = jnp.where(live_mask, jnp.exp(scores - row_max[..., None]), 0.0)
    row_sum = jnp.sum(weights, axis=3)
    mixed = jnp.einsum(
        "bhqk,bkhd->bqhd",
        weights.astype(jnp.bfloat16),
        value_set,
        preferred_element_type=jnp.float32,
    )
    attention = (mixed / jnp.transpose(row_sum, (0, 2, 1))[..., None]).astype(jnp.bfloat16)
    block_total = row_max + jnp.log(row_sum)
    block_dot = jnp.sum(g_blocks.astype(jnp.float32) * attention.astype(jnp.float32), axis=3)
    dot_bhq = jnp.transpose(block_dot, (0, 2, 1))
    log_total = jnp.transpose(block_total, (0, 2, 1)).reshape(row_count, heads_here)
    grad_dot = block_dot.reshape(row_count, heads_here)
    k_second, v_second = (
        lax.all_gather(k_rows, "seq", axis=0, tiled=True),
        lax.all_gather(v_rows, "seq", axis=0, tiled=True),
    )
    key_again, value_again = listed_sets(k_second, v_second)
    scores_again = block_scores(key_again)
    probs = jnp.where(live_mask, jnp.exp(scores_again - block_total[..., None]), 0.0)
    dprob = jnp.einsum("bqhd,bkhd->bhqk", g_blocks, value_again, preferred_element_type=jnp.float32)
    dscore = (probs * (dprob - dot_bhq[..., None])).astype(jnp.bfloat16)
    query_acc = jnp.einsum("bhqk,bkhd->bqhd", dscore, key_again, preferred_element_type=jnp.float32)
    all_log_total, all_grad_dot = (
        lax.all_gather(log_total, "seq", axis=0, tiled=True),
        lax.all_gather(grad_dot, "seq", axis=0, tiled=True),
    )
    table = block_table(key_blocks, counts)
    local_hot = one_hot_rows(lax.axis_index("seq") * row_count, row_count, block_count)
    key_table = jnp.einsum("bc,kc->bk", table, local_hot)
    k_heads = k_rows.reshape(row_count, heads_here, head_dim)
    v_heads = v_rows.reshape(row_count, heads_here, head_dim)
    zero_heads = jnp.zeros((row_count, heads_here, head_dim), jnp.float32)
    q_piece = lax.all_gather(q_rows, "seq", axis=0, tiled=True)
    g_piece = lax.all_gather(g_rows, "seq", axis=0, tiled=True)
    piece_rows = q_piece.shape[0]
    tile_rows = math.gcd(piece_rows, tile_limit)

    def tile(tile_index, fold_state):
        offset = tile_index * tile_rows
        q_tile = lax.dynamic_slice_in_dim(q_piece, offset, tile_rows, 0).reshape(
            tile_rows, heads_here, head_dim
        )
        g_tile = lax.dynamic_slice_in_dim(g_piece, offset, tile_rows, 0).reshape(
            tile_rows, heads_here, head_dim
        )
        total_tile = lax.dynamic_slice_in_dim(all_log_total, offset, tile_rows, 0)
        dot_tile = lax.dynamic_slice_in_dim(all_grad_dot, offset, tile_rows, 0)
        query_hot = one_hot_rows(offset, tile_rows, block_count)
        allowed = jnp.einsum("qb,bk->qk", query_hot, key_table) > 0.5
        tile_scores = (
            jnp.einsum("qhd,khd->qhk", q_tile, k_heads, preferred_element_type=jnp.float32)
            * score_scale
        )
        tile_scores = jnp.where(allowed[:, None, :], tile_scores, neg_fill)
        tile_probs = jnp.where(
            allowed[:, None, :], jnp.exp(tile_scores - total_tile[:, :, None]), 0.0
        )
        value_acc = fold_state[1] + jnp.einsum(
            "qhk,qhd->khd",
            tile_probs.astype(jnp.bfloat16),
            g_tile,
            preferred_element_type=jnp.float32,
        )
        tile_dprob = jnp.einsum("qhd,khd->qhk", g_tile, v_heads, preferred_element_type=jnp.float32)
        tile_ds = (tile_probs * (tile_dprob - dot_tile[:, :, None])).astype(jnp.bfloat16)
        key_acc = fold_state[0] + jnp.einsum(
            "qhk,qhd->khd", tile_ds, q_tile, preferred_element_type=jnp.float32
        )
        return (key_acc, value_acc)

    key_acc, value_acc = lax.fori_loop(0, piece_rows // tile_rows, tile, (zero_heads, zero_heads))
    query_grad = (query_acc * score_scale).astype(jnp.bfloat16).reshape(row_count, feat_width)
    key_grad = (key_acc * score_scale).astype(jnp.bfloat16).reshape(row_count, feat_width)
    value_grad = value_acc.astype(jnp.bfloat16).reshape(row_count, feat_width)
    return (attention.reshape(row_count, feat_width), query_grad, key_grad, value_grad)


def solution(mesh):
    in_specs = (
        P(("seq", "head"), None),
        P(("seq", "head"), None),
        P(("seq", "head"), None),
        P(("seq", "head"), None),
        P(),
        P(),
    )
    out_specs = (P("seq", "head"), P("seq", "head"), P("seq", "head"), P("seq", "head"))
    return jax.shard_map(
        on_device, mesh=mesh, in_specs=in_specs, out_specs=out_specs, check_vma=False
    )
```

profile of v0, /device:TPU:8, one launch (start us, length us, event | category | flops | bytes accessed | tf_op | source)
XLA Modules:
  0.0 496.2 jit_solution(53246647357267488)
XLA Ops:
  8.1 9.9 %all_to_all.76 = bf16[64,8,128]{2,0,1:T(8,128)(2,1)} all-to-all(bf16[64,8,128]{2,0,1:T(8,128)(2,1)S(1)} %copy_bitcast_fusion.2), channel_id=1, replica_groups=mesh['seq'=32,'head'=8] {'head'}, dimensions={1} | all-to-all | bytes 262144 | tf_op jit(solution)/shard_map/all_to_all | solution.py:32
  19.0 9.2 %all_to_all.77 = bf16[64,8,128]{2,0,1:T(8,128)(2,1)} all-to-all(bf16[64,8,128]{2,0,1:T(8,128)(2,1)S(1)} %copy_bitcast_fusion.3), channel_id=1, replica_groups=mesh['seq'=32,'head'=8] {'head'}, dimensions={1} | all-to-all | bytes 262144 | tf_op jit(solution)/shard_map/all_to_all | solution.py:33
  29.1 9.2 %all_to_all.78 = bf16[64,8,128]{2,0,1:T(8,128)(2,1)} all-to-all(bf16[64,8,128]{2,0,1:T(8,128)(2,1)S(1)} %copy_bitcast_fusion.1), channel_id=1, replica_groups=mesh['seq'=32,'head'=8] {'head'}, dimensions={1} | all-to-all | bytes 262144 | tf_op jit(solution)/shard_map/all_to_all | solution.py:31
  39.3 9.2 %all_to_all.79 = bf16[64,8,128]{2,0,1:T(8,128)(2,1)} all-to-all(bf16[64,8,128]{2,0,1:T(8,128)(2,1)S(1)} %copy_bitcast_fusion), channel_id=1, replica_groups=mesh['seq'=32,'head'=8] {'head'}, dimensions={1} | all-to-all | bytes 262144 | tf_op jit(solution)/shard_map/all_to_all | solution.py:34
  50.0 51.3 %all-gather.7.cloned.1.call-done = bf16[16384,128]{1,0:T(8,128)(2,1)} async-done(((bf16[512,128]{1,0:T(8,128)(2,1)}), bf16[16384,128]{1,0:T(8,128)(2,1)}) %all-gather.7.cloned.1.call-update) | async-done | bytes 4194320 | tf_op jit(solution)/shard_map/all_gather | solution.py:72
  101.3 2.9 gather_fusion.1
  104.3 78.2 %all-gather.5.cloned.1.call-done = bf16[16384,128]{1,0:T(8,128)(2,1)} async-done(((bf16[512,128]{1,0:T(8,128)(2,1)}), bf16[16384,128]{1,0:T(8,128)(2,1)}) %all-gather.5.cloned.1.call-update) | async-done | bytes 4194320 | tf_op jit(solution)/shard_map/all_gather | solution.py:73
  182.5 2.9 gather_fusion
  188.5 47.6 %all_gather.23 = f32[16384,1]{0,1:T(1,128)S(1)} all-gather(f32[512,1]{0,1:T(1,128)S(1)} %bitcast.245), channel_id=1, replica_groups=mesh['seq'=32,'head'=8] {'seq'}, dimensions={0}, use_global_device_ids=true | all-gather | bytes 67584 | tf_op jit(solution)/shard_map/all_gather | solution.py:103
  236.1 2.7 fusion.54
  238.8 47.4 %all_gather.25 = f32[16384,1]{0,1:T(1,128)S(1)} all-gather(f32[512,1]{0,1:T(1,128)S(1)} %bitcast.246), channel_id=1, replica_groups=mesh['seq'=32,'head'=8] {'seq'}, dimensions={0}, use_global_device_ids=true | all-gather | bytes 67584 | tf_op jit(solution)/shard_map/all_gather | solution.py:104
  286.1 3.5 fusion.41
  289.6 55.2 %all-gather.11.cloned.1.call-done = bf16[16384,128]{1,0:T(8,128)(2,1)} async-done(((bf16[512,128]{1,0:T(8,128)(2,1)}), bf16[16384,128]{1,0:T(8,128)(2,1)}) %all-gather.11.cloned.1.call-update) | async-done | bytes 4194320 | tf_op jit(solution)/shard_map/all_gather | solution.py:113
  344.8 143.3 %while.18 = (s32[]{:T(128)}, f32[512,1,128]{0,2,1:T(8,128)S(1)}, f32[512,1,128]{0,2,1:T(8,128)S(1)}, bf16[16384,128]{1,0:T(8,128)(2,1)}, bf16[128,512]{1,0:T(8,1...) while((s32[]{:T(128)}, f32[512,1,128]{0,2,1:T(8,128)S(1)}, ...), condition=%wide.region_5.7_spmd.clone, body=%wide.region_4.6_spmd.clone.sunk | while | flops 338239488 | bytes 5654229 | solution.py:150
  346.6 1.5 fusion.97
  355.5 1.5 fusion.97
  360.0 1.5 fusion.97
  369.0 1.5 fusion.97
  373.5 1.5 fusion.97
  382.4 1.5 fusion.97
  395.8 1.5 fusion.97
  409.3 1.5 fusion.97
  422.7 1.5 fusion.97
  427.2 1.5 fusion.97
  436.1 1.5 fusion.97
  440.6 1.5 fusion.97
  449.6 1.5 fusion.97
  454.0 1.5 fusion.97
  463.0 1.5 fusion.97
  467.5 1.5 fusion.97
  476.4 1.5 fusion.97
  480.9 1.5 fusion.97
  (228 shorter events, 124.0 us)
Async XLA Ops:
  7.2 0.9 copy-start
  7.2 41.3 %copy-start.7 = (s32[128,8]{0,1:T(8,128)S(1)}, s32[128,8]{0,1:T(8,128)}, u32[]{:S(2)}) copy-start(s32[128,8]{0,1:T(8,128)} %param.14) | copy-start | bytes 12292
  7.2 41.8 %copy-start.8 = (s32[128]{0:T(128)S(1)}, s32[128]{0:T(128)}, u32[]{:S(2)}) copy-start(s32[128]{0:T(128)} %param.15) | copy-start | bytes 1540
  7.2 94.1 %all-gather.7.cloned.1.call-start = ((), (), s32[]{:S(2)}) async-start(), calls=%async_computation.5 | async-start | bytes 4325376 | tf_op jit(solution)/shard_map/all_gather | solution.py:72
  18.0 164.5 %all-gather.5.cloned.1.call-start = ((), (), s32[]{:S(2)}) async-start(), calls=%async_computation.4 | async-start | bytes 4325376 | tf_op jit(solution)/shard_map/all_gather | solution.py:73
  28.2 261.5 %all-gather.9.cloned.1.call-start = ((), (), s32[]{:S(2)}) async-start(), calls=%async_computation.6 | async-start | bytes 4325376 | tf_op jit(solution)/shard_map/all_gather | solution.py:112
  38.3 306.5 %all-gather.11.cloned.1.call-start = ((), (), s32[]{:S(2)}) async-start(), calls=%async_computation.7 | async-start | bytes 4325376 | tf_op jit(solution)/shard_map/all_gather | solution.py:113
  185.4 0.9 copy-start.5
  185.7 2.7 copy-start.2
  185.7 50.3 %copy-start.3 = (bf16[4,8,128,1,128]{4,2,1,0,3:T(8,128)(2,1)}, bf16[4,8,128,1,128]{4,2,1,0,3:T(8,128)(2,1)S(1)}, u32[]{:S(2)}) copy-start(bf16[4,8,128,1,128]{4,2,1,0,3:T(8,128)(2,1)S(1)} %get-tuple-element.309) | copy-start | bytes 3145732
  186.3 49.7 %copy-start.6 = (bf16[64,8,128]{2,0,1:T(8,128)(2,1)S(1)}, bf16[64,8,128]{2,0,1:T(8,128)(2,1)}, u32[]{:S(2)}) copy-start(bf16[64,8,128]{2,0,1:T(8,128)(2,1)} %all_to_all.79) | copy-start | bytes 393220
  286.1 58.7 %copy-start.1 = (bf16[64,8,128]{2,0,1:T(8,128)(2,1)S(1)}, bf16[64,8,128]{2,0,1:T(8,128)(2,1)}, u32[]{:S(2)}) copy-start(bf16[64,8,128]{2,0,1:T(8,128)(2,1)} %all_to_all.77) | copy-start | bytes 393220
  286.1 58.7 %copy-start.4 = (bf16[64,8,128]{2,0,1:T(8,128)(2,1)S(1)}, bf16[64,8,128]{2,0,1:T(8,128)(2,1)}, u32[]{:S(2)}) copy-start(bf16[64,8,128]{2,0,1:T(8,128)(2,1)} %all_to_all.76) | copy-start | bytes 393220
Sparse Core Ops, SparseCore 0:
  18.1 83.1 all-gather.6
  103.9 78.5 all-gather.4
  185.1 78.5 all-gather.8
  266.1 78.6 all-gather.10
where the time goes:
time: 498 us; the launch traced here: 496 us
  waiting for transfers between devices  185 us (37%)
  matrix products  148 us (30%)
  blocking collectives  132 us (27%)
  between operations  14 us (3%)
  local copies, waits for them, and re-layouts  11.9 us (2%)
    all_gather x1, waiting for transfers between devices, on_device(): lax.all_gather(v_rows, 'seq', axis=0, tiled=True)  78.2 us
    all_gather x1, waiting for transfers between devices, on_device(): g_piece = lax.all_gather(g_rows, 'seq', axis=0, tiled=True)  55.2 us
    all_gather x1, waiting for transfers between devices, on_device(): lax.all_gather(k_rows, 'seq', axis=0, tiled=True)  51.3 us
    dot_general x32, matrix products, tile(): jnp.einsum('qhk,qhd->khd', tile_ds, q_tile, preferred_element_type=jnp.fl...  47.7 us
    all_gather x1, blocking collectives, on_device(): lax.all_gather(log_total, 'seq', axis=0, tiled=True)  47.6 us
    all_gather x1, blocking collectives, on_device(): lax.all_gather(grad_dot, 'seq', axis=0, tiled=True)  47.4 us
    dot_general x32, matrix products, tile(): jnp.einsum('qhd,khd->qhk', q_tile, k_heads, preferred_element_type=jnp.fl...  43.6 us
    dot_general x32, matrix products, tile(): jnp.einsum('qhk,qhd->khd', tile_probs.astype(jnp.bfloat16), g_tile, prefe...  37.8 us
  transfers between devices with their start and end apart: 4, of which 3 were waited for; matrix products, arithmetic and copies ran while one was open for 4% of the time, Pallas kernels for 0%

commit v1 on v0

--- a/solution.py
+++ b/solution.py
@@ -3,11 +3,18 @@
 import jax.numpy as jnp
 from jax import lax
 from jax.sharding import PartitionSpec as P
+from jax.lax import all_gather
 
 HEADS = 8
 BLK = 128
 neg_fill = -1e30
 tile_limit = 512
+
+
+def serve_steps_all(x_part, arr_in, bus_axis):
+    block_now = jnp.concatenate([x_part, arr_in], axis=1)
+    moved = all_gather(block_now, bus_axis, axis=0, tiled=True)
+    return jnp.split(moved, [x_part.shape[1]], axis=1)
 
 
 def block_table(key_blocks, counts):
@@ -109,8 +116,7 @@
     k_heads = k_rows.reshape(row_count, heads_here, head_dim)
     v_heads = v_rows.reshape(row_count, heads_here, head_dim)
     zero_heads = jnp.zeros((row_count, heads_here, head_dim), jnp.float32)
-    q_piece = lax.all_gather(q_rows, "seq", axis=0, tiled=True)
-    g_piece = lax.all_gather(g_rows, "seq", axis=0, tiled=True)
+    q_piece, g_piece = serve_steps_all(q_rows, arr_in=g_rows, bus_axis="seq")
     piece_rows = q_piece.shape[0]
     tile_rows = math.gcd(piece_rows, tile_limit)
 

time: 498 us -> 449 us (0.902)
  waiting for transfers between devices: 185 us -> 133 us
  blocking collectives: 132 us -> 123 us
  local copies, waits for them, and re-layouts: 11.9 us -> 17.6 us
    all_gather x2 -> x1, waiting for transfers between devices: 55.2 us -> 0.01 us  [serve_steps_all(): moved = all_gather(block_now, bus_axis, axis=0, tiled=True)]
    all_to_all x1 -> x0, blocking collectives: 9.16 us -> none  [on_device(): lax.all_to_all(out_grad, 'head', split_axis=1, concat_axis=0, tiled=True)]
    split x0 -> x1, local copies, waits for them, and re-layouts: none -> 5.74 us  [serve_steps_all(): return jnp.split(moved, [x_part.shape[1]], axis=1)]
where the time goes in v1:
time: 449 us; the launch traced here: 447 us
  matrix products  148 us (33%)
  waiting for transfers between devices  133 us (30%)
  blocking collectives  123 us (27%)
  local copies, waits for them, and re-layouts  17.6 us (4%)
  between operations  13.9 us (3%)
  starting transfers between devices  4.82 us (1%)
    all_gather x1, waiting for transfers between devices, on_device(): lax.all_gather(v_rows, 'seq', axis=0, tiled=True)  78.2 us
    all_gather x1, waiting for transfers between devices, on_device(): lax.all_gather(k_rows, 'seq', axis=0, tiled=True)  51.5 us
    all_gather x1, blocking collectives, on_device(): lax.all_gather(grad_dot, 'seq', axis=0, tiled=True)  48.3 us
    dot_general x32, matrix products, tile(): jnp.einsum('qhk,qhd->khd', tile_ds, q_tile, preferred_element_type=jnp.fl...  47.7 us
    all_gather x1, blocking collectives, on_device(): lax.all_gather(log_total, 'seq', axis=0, tiled=True)  47.6 us
    dot_general x32, matrix products, tile(): jnp.einsum('qhd,khd->qhk', q_tile, k_heads, preferred_element_type=jnp.fl...  43.6 us
    dot_general x32, matrix products, tile(): jnp.einsum('qhk,qhd->khd', tile_probs.astype(jnp.bfloat16), g_tile, prefe...  37.8 us
    dot_general x32, matrix products, tile(): allowed = jnp.einsum('qb,bk->qk', query_hot, key_table) > 0.5  11.2 us
  transfers between devices with their start and end apart: 4, of which 3 were waited for; matrix products, arithmetic and copies ran while one was open for 4% of the time, Pallas kernels for 0%

profile of v1, /device:TPU:8, one launch (start us, length us, event | category | flops | bytes accessed | tf_op | source)
XLA Modules:
  0.0 447.0 jit_solution(11789927174313754574)
XLA Ops:
  8.1 9.9 %all_to_all.76 = bf16[64,8,128]{2,0,1:T(8,128)(2,1)} all-to-all(bf16[64,8,128]{2,0,1:T(8,128)(2,1)S(1)} %copy_bitcast_fusion.2), channel_id=1, replica_groups=mesh['seq'=32,'head'=8] {'head'}, dimensions={1} | all-to-all | bytes 262144 | tf_op jit(solution)/shard_map/all_to_all | solution.py:39
  19.0 9.2 %all_to_all.77 = bf16[64,8,128]{2,0,1:T(8,128)(2,1)} all-to-all(bf16[64,8,128]{2,0,1:T(8,128)(2,1)S(1)} %copy_bitcast_fusion.3), channel_id=1, replica_groups=mesh['seq'=32,'head'=8] {'head'}, dimensions={1} | all-to-all | bytes 262144 | tf_op jit(solution)/shard_map/all_to_all | solution.py:40
  28.2 1.6 copy_bitcast_fusion
  29.7 4.7 %all-to-all-start.3 = ((bf16[64,8,128]{2,0,1:T(8,128)(2,1)}), bf16[64,8,128]{2,0,1:T(8,128)(2,1)S(1)}, u32[]{:S(2)}, u32[]{:S(2)}) async-start(bf16[64,8,128]{2,0,1:T(8,128)(2,1)} %copy_bitcast_fusion), calls=%async_computation.3 | async-start | bytes 262144 | tf_op jit(solution)/shard_map/all_to_all | solution.py:41
  35.4 3.7 all-to-all-done.3
  39.2 8.5 %all_to_all.78 = bf16[64,8,128]{2,0,1:T(8,128)(2,1)S(1)} all-to-all(bf16[64,8,128]{2,0,1:T(8,128)(2,1)S(1)} %copy_bitcast_fusion.1), channel_id=1, replica_groups=mesh['seq'=32,'head'=8] {'head'}, dimensions={1} | all-to-all | bytes 262144 | tf_op jit(solution)/shard_map/all_to_all | solution.py:38
  49.9 51.5 %all-gather.6.cloned.1.call-done = bf16[16384,128]{1,0:T(8,128)(2,1)} async-done(((bf16[512,128]{1,0:T(8,128)(2,1)}), bf16[16384,128]{1,0:T(8,128)(2,1)}) %all-gather.6.cloned.1.call-update) | async-done | bytes 4194320 | tf_op jit(solution)/shard_map/all_gather | solution.py:79
  101.4 2.9 gather_fusion.1
  104.3 78.2 %all-gather.4.cloned.1.call-done = bf16[16384,128]{1,0:T(8,128)(2,1)} async-done(((bf16[512,128]{1,0:T(8,128)(2,1)}), bf16[16384,128]{1,0:T(8,128)(2,1)}) %all-gather.4.cloned.1.call-update) | async-done | bytes 4194320 | tf_op jit(solution)/shard_map/all_gather | solution.py:80
  182.5 2.9 gather_fusion
  187.9 47.6 %all_gather.20 = f32[16384,1]{0,1:T(1,128)S(1)} all-gather(f32[512,1]{0,1:T(1,128)S(1)} %bitcast.245), channel_id=1, replica_groups=mesh['seq'=32,'head'=8] {'seq'}, dimensions={0}, use_global_device_ids=true | all-gather | bytes 67584 | tf_op jit(solution)/shard_map/all_gather | solution.py:110
  235.5 2.7 fusion.54
  238.2 48.3 %all_gather.21 = f32[16384,1]{0,1:T(1,128)S(1)} all-gather(f32[512,1]{0,1:T(1,128)S(1)} %bitcast.246), channel_id=1, replica_groups=mesh['seq'=32,'head'=8] {'seq'}, dimensions={0}, use_global_device_ids=true | all-gather | bytes 67584 | tf_op jit(solution)/shard_map/all_gather | solution.py:111
  286.4 3.4 fusion.41
  289.8 5.7 %fusion.63 = (bf16[16384,128]{1,0:T(8,128)(2,1)}, bf16[16384,128]{1,0:T(8,128)(2,1)}) fusion(bf16[16384,256]{1,0:T(8,128)(2,1)} %all-gather.8.cloned.1.call-done), kind=kLoop, calls=%fused_computation.107 | loop fusion | bytes 16777216 | tf_op jit(solution)/shard_map/split | solution.py:17
  295.6 143.3 %while.18 = (s32[]{:T(128)}, f32[512,1,128]{0,2,1:T(8,128)S(1)}, f32[512,1,128]{0,2,1:T(8,128)S(1)}, bf16[16384,128]{1,0:T(8,128)(2,1)}, bf16[128,512]{1,0:T(8,1...) while((s32[]{:T(128)}, f32[512,1,128]{0,2,1:T(8,128)S(1)}, ...), condition=%wide.region_5.7_spmd.clone, body=%wide.region_4.6_spmd.clone.sunk | while | flops 338239488 | bytes 5654229 | solution.py:156
  297.4 1.5 fusion.98
  301.9 1.5 fusion.98
  310.8 1.5 fusion.98
  315.3 1.5 fusion.98
  324.2 1.5 fusion.98
  328.7 1.5 fusion.98
  337.7 1.5 fusion.98
  342.2 1.5 fusion.98
  351.1 1.5 fusion.98
  355.6 1.5 fusion.98
  364.5 1.5 fusion.98
  378.0 1.5 fusion.98
  391.4 1.5 fusion.98
  404.8 1.5 fusion.98
  418.3 1.5 fusion.98
  431.7 1.5 fusion.98
  (224 shorter events, 126.0 us)
Async XLA Ops:
  7.2 0.9 copy-start
  7.2 41.2 %copy-start.5 = (s32[128,8]{0,1:T(8,128)S(1)}, s32[128,8]{0,1:T(8,128)}, u32[]{:S(2)}) copy-start(s32[128,8]{0,1:T(8,128)} %param.14) | copy-start | bytes 12292
  7.2 41.7 %copy-start.6 = (s32[128]{0:T(128)S(1)}, s32[128]{0:T(128)}, u32[]{:S(2)}) copy-start(s32[128]{0:T(128)} %param.15) | copy-start | bytes 1540
  7.2 94.2 %all-gather.6.cloned.1.call-start = ((), (), s32[]{:S(2)}) async-start(), calls=%async_computation.5 | async-start | bytes 4325376 | tf_op jit(solution)/shard_map/all_gather | solution.py:79
  18.0 164.5 %all-gather.4.cloned.1.call-start = ((), (), s32[]{:S(2)}) async-start(), calls=%async_computation.4 | async-start | bytes 4325376 | tf_op jit(solution)/shard_map/all_gather | solution.py:80
  29.7 9.4 %all-to-all-start.3 = ((bf16[64,8,128]{2,0,1:T(8,128)(2,1)}), bf16[64,8,128]{2,0,1:T(8,128)(2,1)S(1)}, u32[]{:S(2)}, u32[]{:S(2)}) async-start(bf16[64,8,128]{2,0,1:T(8,128)(2,1)} %copy_bitcast_fusion), calls=%async_computation.3 | async-start | bytes 262144 | tf_op jit(solution)/shard_map/all_to_all | solution.py:41
  34.5 255.4 %all-gather.8.cloned.1.call-start = ((), (), s32[]{:S(2)}) async-start(), calls=%async_computation.6 | async-start | bytes 8650752 | tf_op jit(solution)/shard_map/all_gather | solution.py:16
  185.7 2.1 copy-start.2
  185.7 49.7 %copy-start.3 = (bf16[4,8,128,1,128]{4,2,1,0,3:T(8,128)(2,1)}, bf16[4,8,128,1,128]{4,2,1,0,3:T(8,128)(2,1)S(1)}, u32[]{:S(2)}) copy-start(bf16[4,8,128,1,128]{4,2,1,0,3:T(8,128)(2,1)S(1)} %get-tuple-element.311) | copy-start | bytes 3145732
  289.8 5.8 %copy-start.1 = (bf16[64,8,128]{2,0,1:T(8,128)(2,1)S(1)}, bf16[64,8,128]{2,0,1:T(8,128)(2,1)}, u32[]{:S(2)}) copy-start(bf16[64,8,128]{2,0,1:T(8,128)(2,1)} %all_to_all.77) | copy-start | bytes 393220
  289.8 5.8 %copy-start.4 = (bf16[64,8,128]{2,0,1:T(8,128)(2,1)S(1)}, bf16[64,8,128]{2,0,1:T(8,128)(2,1)}, u32[]{:S(2)}) copy-start(bf16[64,8,128]{2,0,1:T(8,128)(2,1)} %all_to_all.76) | copy-start | bytes 393220
Sparse Core Ops, SparseCore 0:
  18.1 83.2 all-gather.5
  103.9 78.5 all-gather.3
  185.1 94.9 all-gather.7
